TPU v7x, 256 devices: a whole 4x4x8 slice. The times are simulated.
256 devices in a mesh: seq: 32 (over z, y), ffn: 8 (over x, core).
Axes of the slice: x: 4, y: 4, z: 8, core: 2. Of those that a mesh axis runs over, the one named last changes fastest.
Arguments:
- patches: bfloat16 [8192, 4096], P('seq'), may hold values from -100 to 100
- gate_weight: bfloat16 [4096, 7168], P('seq', 'ffn'), may hold values from -0.09375 to 0.09375
- up_weight: bfloat16 [4096, 7168], P('seq', 'ffn'), may hold values from -0.09375 to 0.09375
- down_weight: bfloat16 [4096, 7168], P('seq', 'ffn'), may hold values from -0.25 to 0.25
- key_weight: bfloat16 [4096, 1024], P(None, 'ffn'), may hold values from -0.09375 to 0.09375
- value_weight: bfloat16 [4096, 1024], P(None, 'ffn'), may hold values from -0.09375 to 0.09375
- byte_states: bfloat16 [65536, 1024], P('seq'), may hold values from -60 to 60
- byte_patch: int32 [65536], P('seq'), may hold values from 0 to 8191, as said below
- cross_query: bfloat16 [1024, 1024], P(None, 'ffn'), may hold values from -0.375 to 0.375
- self_query: bfloat16 [1024, 1024], P(None, 'ffn'), may hold values from -0.375 to 0.375
- self_key: bfloat16 [1024, 1024], P(None, 'ffn'), may hold values from -0.375 to 0.375
- self_value: bfloat16 [1024, 1024], P(None, 'ffn'), may hold values from -0.1875 to 0.1875
- cross_out: bfloat16 [1024, 1024], P('ffn'), may hold values from -0.1875 to 0.1875
- self_out: bfloat16 [1024, 1024], P('ffn'), may hold values from -0.1875 to 0.1875
Outputs:
- update: bfloat16 [65536, 1024], P('seq', 'ffn')
Inputs may be any that keep to these rules, and one draw needn't show every extreme that they name: byte_patch starts at 0, never falls, rises by at most 1 from one byte to the next and ends at 8191, so every patch is a run of one or more bytes. The bytes s * 2048 to (s + 1) * 2048 - 1 read only patches s * 256 - 23 to (s + 1) * 256 + 15; both ends are reached in every draw.
All inputs are finite; a program needn't handle non-finite values.
Results may differ from a plain program's by a relative error of at most 0.0085.
The roundings to bfloat16 on the way count: a program that leaves them out, or rounds other values in their place, can miss the bound.
Values may be sent and summed in bfloat16 or wider, within the bound.
No kernel may reach another device: no remote copies, remote signals or barrier semaphores. Data moves between devices by JAX's collectives and lax.ppermute only.
A program may use at most 128 MiB of HBM per device.

v0:
```python
import math
import jax
import jax.numpy as jnp
from jax import lax
from jax.sharding import PartitionSpec as P

HD = 64
PWIN = 8
WINDOW = 512
HALO = 23
EPS = 1e-05


def padded(value, sides, width):
    for axis, dim in sides:
        count, length = (lax.axis_size(axis), value.shape[dim])
        up = [(i, (i + 1) % count) for i in range(count - 1)]
        down = [(j, i) for i, j in up]
        last = lax.slice_in_dim(value, length - width, length, axis=dim)
        first = lax.slice_in_dim(value, 0, width, axis=dim)
        before = lax.ppermute(last, axis, up)
        after = lax.ppermute(first, axis, down)
        value = jnp.concatenate([before, value, after], axis=dim)
    return value


def shifted(value, axis, by):
    count = lax.axis_size(axis)
    pairs = [(i, i + by) for i in range(count) if 0 <= i + by < count]
    return lax.ppermute(value, axis, pairs)


def row_normalize(matrix):
    widened = matrix.astype(jnp.float32)
    return widened * lax.rsqrt(jnp.mean(widened * widened, axis=-1, keepdims=True) + EPS)


def masked_softmax(scores, key_mask):
    masked = jnp.where(key_mask, scores, -jnp.inf)
    row_max = jnp.max(masked, axis=-1, keepdims=True)
    exp_terms = jnp.exp(masked - row_max)
    return exp_terms / jnp.sum(exp_terms, axis=-1, keepdims=True)


def local(
    patches,
    gate_weight,
    up_weight,
    down_weight,
    key_weight,
    value_weight,
    byte_states,
    byte_patch,
    cross_query,
    self_query,
    self_key,
    self_value,
    cross_out,
    self_out,
):
    patch_count = patches.shape[0]
    normed = row_normalize(patches).astype(jnp.bfloat16)

    def add_rows(piece_rows):
        return jnp.dot(normed, piece_rows, preferred_element_type=jnp.float32)

    gate_sum = add_rows(lax.all_gather(gate_weight, "seq", axis=0, tiled=True))
    up_sum = add_rows(lax.all_gather(up_weight, "seq", axis=0, tiled=True))
    hidden = (jax.nn.silu(gate_sum) * up_sum).astype(jnp.bfloat16)
    ffn_out = lax.dot_general(
        hidden,
        lax.all_gather(down_weight, "seq", axis=0, tiled=True),
        (((1,), (1,)), ((), ())),
        preferred_element_type=jnp.float32,
    )
    ffn_whole = lax.psum(ffn_out, "ffn")
    global_out = (patches.astype(jnp.float32) + ffn_whole).astype(jnp.bfloat16)
    head_cols = key_weight.shape[1]
    head_count = head_cols // HD
    score_scale = 1.0 / math.sqrt(HD)
    seq_index = lax.axis_index("seq")
    keys_c = jnp.dot(global_out, key_weight, preferred_element_type=jnp.float32).astype(
        jnp.bfloat16
    )
    values_c = jnp.dot(global_out, value_weight, preferred_element_type=jnp.float32).astype(
        jnp.bfloat16
    )
    both_c = jnp.concatenate([keys_c, values_c], axis=1)
    extended = padded(both_c, (("seq", 0),), HALO)
    key_count = extended.shape[0]
    key_index = seq_index * patch_count - HALO + jnp.arange(key_count, dtype=jnp.int32)
    cross_mask = (
        (key_index[None, :] <= byte_patch[:, None])
        & (key_index[None, :] > byte_patch[:, None] - PWIN)
        & (key_index[None, :] >= 0)
    )
    byte_count = byte_states.shape[0]
    query_c = jnp.dot(byte_states, cross_query, preferred_element_type=jnp.float32).astype(
        jnp.bfloat16
    )
    query_s = jnp.dot(byte_states, self_query, preferred_element_type=jnp.float32).astype(
        jnp.bfloat16
    )
    keys_s = jnp.dot(byte_states, self_key, preferred_element_type=jnp.float32).astype(jnp.bfloat16)
    values_s = jnp.dot(byte_states, self_value, preferred_element_type=jnp.float32).astype(
        jnp.bfloat16
    )
    query_here = query_c.reshape(byte_count, head_count, HD)
    keys_here = extended[:, :head_cols].reshape(key_count, head_count, HD)
    values_here = extended[:, head_cols:].reshape(key_count, head_count, HD)
    cross_scores = (
        jnp.einsum("qhd,khd->hqk", query_here, keys_here, preferred_element_type=jnp.float32)
        * score_scale
    )
    weights_c = masked_softmax(cross_scores, cross_mask[None]).astype(jnp.bfloat16)
    context_c = jnp.einsum(
        "hqk,khd->qhd", weights_c, values_here, preferred_element_type=jnp.float32
    )
    context_c = context_c.astype(jnp.bfloat16).reshape(byte_count, head_cols)
    both_s = jnp.concatenate([keys_s, values_s], axis=1)
    tail_rows = both_s[byte_count - WINDOW :]
    before = shifted(tail_rows, "seq", 1)
    stacked = jnp.concatenate([before, both_s], axis=0)
    blocks = byte_count // WINDOW
    lower_half = stacked[:byte_count].reshape(blocks, WINDOW, 2 * head_cols)
    upper_half = stacked[WINDOW:].reshape(blocks, WINDOW, 2 * head_cols)
    key_pairs = jnp.concatenate([lower_half, upper_half], axis=1)
    window_keys = key_pairs[:, :, :head_cols].reshape(blocks, 2 * WINDOW, head_count, HD)
    window_values = key_pairs[:, :, head_cols:].reshape(blocks, 2 * WINDOW, head_count, HD)
    window_queries = query_s.reshape(blocks, WINDOW, head_count, HD)
    self_scores = (
        jnp.einsum(
            "bqhd,bkhd->bhqk", window_queries, window_keys, preferred_element_type=jnp.float32
        )
        * score_scale
    )
    query_slot = jnp.arange(WINDOW, dtype=jnp.int32)[:, None]
    key_slot = jnp.arange(2 * WINDOW, dtype=jnp.int32)[None, :]
    band_mask = (key_slot > query_slot) & (key_slot <= query_slot + WINDOW)
    block_ids = jnp.arange(blocks, dtype=jnp.int32)
    key_pos = (
        seq_index * byte_count
        - WINDOW
        + block_ids[:, None] * WINDOW
        + jnp.arange(2 * WINDOW, dtype=jnp.int32)[None, :]
    )
    self_mask = band_mask[None, None] & (key_pos >= 0)[:, None, None, :]
    weights_s = masked_softmax(self_scores, self_mask).astype(jnp.bfloat16)
    context_s = jnp.einsum(
        "bhqk,bkhd->bqhd", weights_s, window_values, preferred_element_type=jnp.float32
    )
    context_s = context_s.astype(jnp.bfloat16).reshape(byte_count, head_cols)
    partial_sum = jnp.dot(context_c, cross_out, preferred_element_type=jnp.float32) + jnp.dot(
        context_s, self_out, preferred_element_type=jnp.float32
    )
    return lax.psum_scatter(partial_sum, "ffn", scatter_dimension=1, tiled=True).astype(
        jnp.bfloat16
    )


def solution(mesh):
    placed = (
        P("seq", None),
        P("seq", "ffn"),
        P("seq", "ffn"),
        P("seq", "ffn"),
        P(None, "ffn"),
        P(None, "ffn"),
        P("seq", None),
        P("seq"),
        P(None, "ffn"),
        P(None, "ffn"),
        P(None, "ffn"),
        P(None, "ffn"),
        P("ffn", None),
        P("ffn", None),
    )
    return jax.shard_map(
        local, mesh=mesh, in_specs=placed, out_specs=P("seq", "ffn"), check_vma=False
    )
```

profile of v0, /device:TPU:1, one launch (start us, length us, event | category | flops | bytes accessed | tf_op | source)
XLA Modules:
  0.0 472.8 jit_solution(5095927345951818433)
XLA Ops:
  6.5 0.7 all-gather.4.cloned.1.call-update
  7.3 0.0 all-gather.6.cloned.1.call-start
  7.3 0.7 all-gather.6.cloned.1.call-update
  8.0 0.0 all-gather.8.cloned.1.call-start
  8.1 0.7 all-gather.8.cloned.1.call-update
  8.7 0.0 all-reduce.2.cloned.1.call-start
  8.8 0.0 copy-start.2
  8.8 3.9 convolution_convert_fusion.2
  12.7 0.0 copy-start.16
  12.7 0.0 copy-start.14
  12.7 1.5 convolution_convert_fusion.1
  14.3 0.8 copy-done.7
  15.1 4.7 collective-permute-start.2
  19.9 0.1 add_compare_fusion
  19.9 0.0 copy-done.16
  20.0 0.4 fusion.16
  20.4 4.8 %convolution_convert_fusion.3 = bf16[2048,128]{0,1:T(8,128)(2,1)} fusion(bf16[2048,1024]{1,0:T(8,128)(2,1)} %param.20, bf16[1024,128]{1,0:T(8,128)(2,1)S(1)} %copy-done.14), kind=kOutput, calls=%fused_computation.31 | convolution fusion | flops 537133056 | bytes 4980736 | tf_op jit(solution)/shard_map/dot_general | solution.py:98
  25.1 0.0 copy-done.3
  25.1 3.2 convolution_convert_fusion
  28.3 1.5 and_and_fusion
  29.8 2.3 broadcast_and_fusion
  32.1 0.0 copy-done.4
  32.1 0.5 fusion.7
  32.6 3.4 reshape.197
  36.0 0.0 collective-permute-done.2
  36.0 3.3 pad_maximum_fusion
  39.2 2.6 reshape.191
  41.9 64.2 %all-gather.4.cloned.1.call-done = bf16[4096,896]{1,0:T(8,128)(2,1)} async-done(((bf16[128,896]{1,0:T(8,128)(2,1)}), bf16[4096,896]{1,0:T(8,128)(2,1)}) %all-gather.4.cloned.1.call-update) | async-done | bytes 7340048 | tf_op jit(solution)/shard_map/all_gather | solution.py:67
  106.1 6.4 %fusion.30 = f32[256,896]{1,0:T(8,128)} fusion(bf16[4096,896]{1,0:T(8,128)(2,1)} %all-gather.4.cloned.1.call-done, bf16[256,4096]{1,0:T(8,128)(2,1)S(1)} %copy-done.4, f32[256]{0:T(256)S(1)} %add_rsqrt_fusion), kind=kOutput, calls=%fused_computation.50 | convolution fusion | flops 1882193920 | bytes 10355712 | tf_op jit(solution)/shard_map/dot_general | solution.py:65
  112.5 86.2 %all-gather.6.cloned.1.call-done = bf16[4096,896]{1,0:T(8,128)(2,1)} async-done(((bf16[128,896]{1,0:T(8,128)(2,1)}), bf16[4096,896]{1,0:T(8,128)(2,1)}) %all-gather.6.cloned.1.call-update) | async-done | bytes 7340048 | tf_op jit(solution)/shard_map/all_gather | solution.py:68
  198.8 92.7 %all-gather.8.cloned.1.call-done = bf16[4096,896]{1,0:T(8,128)(2,1)} async-done(((bf16[128,896]{1,0:T(8,128)(2,1)}), bf16[4096,896]{1,0:T(8,128)(2,1)}) %all-gather.8.cloned.1.call-update) | async-done | bytes 7340048 | tf_op jit(solution)/shard_map/all_gather | solution.py:72
  291.4 12.0 %fusion.35 = f32[256,4096]{1,0:T(8,128)} fusion(bf16[4096,896]{1,0:T(8,128)(2,1)} %all-gather.8.cloned.1.call-done, bf16[4096,896]{1,0:T(8,128)(2,1)} %all-gather.6.cloned.1.call-done, f32[256,896]{1,0:T(8,128)} %fusion.30, bf16[256,4096]{1,0:T(8,128)(2,1)S(1)} %copy-done.4, f32[256]{0:T(256)S(1)} %add_rsqrt_fusion), kind=kOutput, calls=%fused_computation.52 | convolution fusion | flops 3762618368 | bytes 21890048 | tf_op jit(solution)/shard_map/dot_general | solution.py:70
  303.4 0.0 all-reduce.2.cloned.1.call-update
  303.5 0.0 reduce-scatter.2.cloned.1.call-start
  303.5 2.6 constant_dynamic-update-slice_fusion.1
  306.1 2.6 reshape.192
  308.8 2.6 constant_dynamic-update-slice_fusion
  311.3 2.6 fusion.51
  313.9 1.4 copy.20
  315.3 1.3 copy.18
  316.6 11.0 %fusion.54 = (f32[4,2,512]{2,1,0:T(2,128)S(1)}, f32[4,2,512,1024]{3,2,1,0:T(8,128)}) fusion(pred[4,512,1024]{2,1,0:T(8,128)(4,1)} %broadcast_and_fusion, bf16[4,1024,2,64]{1,3,2,0:T(8,128)(2,1)} %bitcast.47, bf16[4,512,2,64]{3,2,1,0:T(2,128)(2,1)} %reshape.197), kind=kOutput, calls=%fused_computation.79 | convolution fusion | flops 553649152 | bytes 20463616 | tf_op jit(solution)/shard_map/sub | solution.py:41
  327.6 49.4 %all-reduce.2.cloned.1.call-done = f32[256,4096]{1,0:T(8,128)} async-done(((f32[256,4096]{1,0:T(8,128)}), f32[256,4096]{1,0:T(8,128)}) %all-reduce.2.cloned.1.call-update) | async-done | bytes 4194320 | tf_op jit(solution)/shard_map/psum | solution.py:76
  377.0 3.1 convolution_convert_fusion.4
  380.2 0.3 copy-done.5
  380.5 0.3 copy-done.8
  380.8 0.9 convolution_convert_fusion.5
  381.6 0.1 fusion.39
  381.7 3.1 collective-permute-start
  384.8 1.6 collective-permute-start.1
  386.4 0.0 copy-start.11
  386.4 8.6 %fusion.21 = bf16[4,512,2,64]{1,3,2,0:T(8,128)(2,1)S(1)} fusion(bf16[4,1024,2,64]{1,3,2,0:T(8,128)(2,1)S(1)} %bitcast.46, f32[4,2,512,1024]{3,2,1,0:T(8,128)} %get-tuple-element.14, f32[4,2,512]{2,1,0:T(2,128)S(1)} %get-tuple-element.13), kind=kOutput, calls=%fused_computation.39 | convolution fusion | flops 545521664 | bytes 18366464 | tf_op jit(solution)/shard_map/bhqk,bkhd->bqhd/dot_general | solution.py:149
  395.0 0.4 copy.22
  395.4 0.1 copy.25
  395.5 0.0 collective-permute-done
  395.6 0.0 collective-permute-done.1
  395.6 0.1 pad_maximum_fusion.3
  395.8 1.8 fusion.53
  397.6 2.5 fusion.15
  400.2 0.0 copy-start.12
  400.2 1.3 fusion.59
  401.5 4.5 convolution_add_fusion
  406.0 0.0 reduce-scatter.2.cloned.1.call-update
  406.0 58.2 %reduce-scatter.2.cloned.1.call-done = f32[2048,128]{1,0:T(8,128)} async-done(((f32[2048,1024]{1,0:T(8,128)}), f32[2048,128]{1,0:T(8,128)}) %reduce-scatter.2.cloned.1.call-update) | async-done | bytes 1048592 | tf_op jit(solution)/shard_map/reduce_scatter | solution.py:156
  464.2 2.1 convert_element_type.68
  (32 shorter events, 0.1 us)
Async XLA Ops:
  6.5 370.5 %copy-start = (bf16[4096,128]{1,0:T(8,128)(2,1)S(1)}, bf16[4096,128]{1,0:T(8,128)(2,1)}, u32[]{:S(2)}) copy-start(bf16[4096,128]{1,0:T(8,128)(2,1)} %param.19) | copy-start | bytes 3145732
  6.5 6.1 %copy-start.13 = (bf16[1024,128]{1,0:T(8,128)(2,1)S(1)}, bf16[1024,128]{1,0:T(8,128)(2,1)}, u32[]{:S(2)}) copy-start(bf16[1024,128]{1,0:T(8,128)(2,1)} %param.25) | copy-start | bytes 786436
  6.5 99.6 %all-gather.4.cloned.1.call-start = ((), (), s32[]{:S(2)}) async-start(), calls=%async_computation.1 | async-start | bytes 7569408 | tf_op jit(solution)/shard_map/all_gather | solution.py:67
  7.3 191.5 %all-gather.6.cloned.1.call-start = ((), (), s32[]{:S(2)}) async-start(), calls=%async_computation.2 | async-start | bytes 7569408 | tf_op jit(solution)/shard_map/all_gather | solution.py:68
  8.0 283.4 %all-gather.8.cloned.1.call-start = ((), (), s32[]{:S(2)}) async-start(), calls=%async_computation.3 | async-start | bytes 7569408 | tf_op jit(solution)/shard_map/all_gather | solution.py:72
  8.7 368.3 %all-reduce.2.cloned.1.call-start = ((), (), s32[]{:S(2)}) async-start(), calls=%async_computation.4 | async-start | bytes 8388608 | tf_op jit(solution)/shard_map/psum | solution.py:76
  8.8 3.9 copy-start.2
  12.7 1.6 copy-start.6
  12.7 7.2 %copy-start.16 = (s32[2048]{0:T(1024)S(1)}, s32[2048]{0:T(1024)}, u32[]{:S(2)}) copy-start(s32[2048]{0:T(1024)} %param.21) | copy-start | bytes 24580
  12.7 7.6 %copy-start.14 = (bf16[1024,128]{1,0:T(8,128)(2,1)S(1)}, bf16[1024,128]{1,0:T(8,128)(2,1)}, u32[]{:S(2)}) copy-start(bf16[1024,128]{1,0:T(8,128)(2,1)} %param.22) | copy-start | bytes 786436
  14.3 0.8 copy-start.7
  15.1 20.8 %collective-permute-start.2 = (bf16[512,256]{0,1:T(8,128)(2,1)S(1)}, bf16[512,256]{0,1:T(8,128)(2,1)}, u32[]{:S(2)}, u32[]{:S(2)}) collective-permute-start(bf16[512,256]{0,1:T(8,128)(2,1)S(1)} %fusion.38), channel_id=1, source_target_pairs={{0,8},{8,16},{16,24},{24,32},{32,40},{40,48},{48,56},{56,64},{64,7... | collective-permute-start | bytes 786440 | tf_op jit(solution)/shard_map/ppermute | solution.py:30
  19.8 5.3 %copy-start.3 = (bf16[2048,1024]{1,0:T(8,128)(2,1)S(1)}, bf16[2048,1024]{1,0:T(8,128)(2,1)}, u32[]{:S(2)}) copy-start(bf16[2048,1024]{1,0:T(8,128)(2,1)} %param.20) | copy-start | bytes 12582916
  25.1 7.0 %copy-start.4 = (bf16[256,4096]{1,0:T(8,128)(2,1)S(1)}, bf16[256,4096]{1,0:T(8,128)(2,1)}, u32[]{:S(2)}) copy-start(bf16[256,4096]{1,0:T(8,128)(2,1)} %param.14) | copy-start | bytes 6291460
  303.5 160.7 %reduce-scatter.2.cloned.1.call-start = ((), (), s32[]{:S(2)}) async-start(), calls=%async_computation.5 | async-start | bytes 9437184 | tf_op jit(solution)/shard_map/reduce_scatter | solution.py:156
  377.0 3.4 copy-start.5
  377.0 3.7 copy-start.8
  380.8 5.7 %copy-start.9 = (bf16[4,1024,128]{1,2,0:T(8,128)(2,1)S(1)}, bf16[4,1024,128]{1,2,0:T(8,128)(2,1)}, u32[]{:S(2)}) copy-start(bf16[4,1024,128]{1,2,0:T(8,128)(2,1)} %copy.18) | copy-start | bytes 3145732
  381.7 13.8 %collective-permute-start = (bf16[23,256]{0,1:T(8,128)(2,1)S(1)}, bf16[23,256]{0,1:T(8,128)(2,1)S(1)}, u32[]{:S(2)}, u32[]{:S(2)}) collective-permute-start(bf16[23,256]{0,1:T(8,128)(2,1)S(1)} %get-tuple-element.11), channel_id=1, source_target_pairs={{0,8},{8,16},{16,24},{24,32},{32,40},{40,48},{48,56},{56,64},{64,7... | collective-permute-start | bytes 35336 | tf_op jit(solution)/shard_map/ppermute | solution.py:21
  384.8 10.7 %collective-permute-start.1 = (bf16[23,256]{0,1:T(8,128)(2,1)S(1)}, bf16[23,256]{0,1:T(8,128)(2,1)S(1)}, u32[]{:S(2)}, u32[]{:S(2)}) collective-permute-start(bf16[23,256]{0,1:T(8,128)(2,1)S(1)} %get-tuple-element.12), channel_id=1, source_target_pairs={{8,0},{16,8},{24,16},{32,24},{40,32},{48,40},{56,48},{64,56},{72,6... | collective-permute-start | bytes 35336 | tf_op jit(solution)/shard_map/ppermute | solution.py:22
  386.4 9.3 %copy-start.10 = (pred[2048,302]{0,1:T(8,128)(4,1)S(1)}, pred[2048,302]{0,1:T(8,128)(4,1)}, u32[]{:S(2)}) copy-start(pred[2048,302]{0,1:T(8,128)(4,1)} %and_and_fusion) | copy-start | bytes 1855492
  386.4 9.3 %copy-start.11 = (bf16[2048,128]{0,1:T(8,128)(2,1)S(1)}, bf16[2048,128]{0,1:T(8,128)(2,1)}, u32[]{:S(2)}) copy-start(bf16[2048,128]{0,1:T(8,128)(2,1)} %convolution_convert_fusion.3) | copy-start | bytes 1572868
  397.6 2.5 copy-start.15
  400.2 1.3 copy-start.12
  406.0 60.3 %copy-start.1 = (bf16[4096,128]{1,0:T(8,128)(2,1)S(1)}, bf16[4096,128]{1,0:T(8,128)(2,1)}, u32[]{:S(2)}) copy-start(bf16[4096,128]{1,0:T(8,128)(2,1)} %param.19) | copy-start | bytes 3145732
Sparse Core Ops, SparseCore 0:
  9.9 96.1 all-gather.3
  108.7 90.0 all-gather.5
  201.3 90.0 all-gather.7
  303.6 73.3 all-reduce.1
  406.1 58.0 reduce-scatter.1
where the time goes:
time: 473 us
  waiting for transfers between devices  353 us (75%)
  matrix products  65.5 us (14%)
  local copies, waits for them, and re-layouts  21.1 us (4%)
  between operations  13.5 us (3%)
  other arithmetic  10.4 us (2%)
  starting transfers between devices  9.53 us (2%)
    all_gather x1, waiting for transfers between devices, local(): lax.all_gather(down_weight, 'seq', axis=0, tiled=True)  92.7 us
    all_gather x1, waiting for transfers between devices, local(): up_sum = add_rows(lax.all_gather(up_weight, 'seq', axis=0, tiled=True))  86.2 us
    all_gather x1, waiting for transfers between devices, local(): gate_sum = add_rows(lax.all_gather(gate_weight, 'seq', axis=0, tiled=True))  64.2 us
    reduce_scatter x1, waiting for transfers between devices, local(): lax.psum_scatter(partial_sum, 'ffn', scatter_dimension=1, tiled=True)  58.2 us
    psum x1, waiting for transfers between devices, local(): ffn_whole = lax.psum(ffn_out, 'ffn')  49.4 us
    sub x2, matrix products, masked_softmax(): exp_terms = jnp.exp(masked - row_max)  12.8 us
    dot_general x1, matrix products, local(): lax.dot_general(hidden, lax.all_gather(down_weight, 'seq', axis=0, tiled=...  12 us
  transfers between devices with their start and end apart: 8, of which 5 were waited for; matrix products, arithmetic and copies ran while one was open for 14% of the time, Pallas kernels for 0%

commit v1 on v0

--- a/solution.py
+++ b/solution.py
@@ -3,6 +3,7 @@
 import jax.numpy as jnp
 from jax import lax
 from jax.sharding import PartitionSpec as P
+from jax.lax import all_gather
 
 HD = 64
 PWIN = 8
@@ -73,7 +74,7 @@
         (((1,), (1,)), ((), ())),
         preferred_element_type=jnp.float32,
     )
-    ffn_whole = lax.psum(ffn_out, "ffn")
+    ffn_whole = all_gather(ffn_out, axis_name="ffn").sum(axis=0)
     global_out = (patches.astype(jnp.float32) + ffn_whole).astype(jnp.bfloat16)
     head_cols = key_weight.shape[1]
     head_count = head_cols // HD

time: 473 us -> 572 us (1.21)
  waiting for transfers between devices: 353 us -> 437 us
  other arithmetic: 10.4 us -> 26.2 us
    all_gather x0 -> x1, waiting for transfers between devices: none -> 104 us  [local(): ffn_whole = all_gather(ffn_out, axis_name='ffn').sum(axis=0)]
    psum x1 -> x0, waiting for transfers between devices: 49.4 us -> none  [local(): ffn_whole = lax.psum(ffn_out, 'ffn')]
    all_gather x1, waiting for transfers between devices: 64.2 us -> 95.2 us  [local(): gate_sum = add_rows(lax.all_gather(gate_weight, 'seq', axis=0, tiled=True))]
    reduce_sum x0 -> x1, other arithmetic: none -> 14.3 us  [local(): ffn_whole = all_gather(ffn_out, axis_name='ffn').sum(axis=0)]
    all_gather x1, waiting for transfers between devices: 92.7 us -> 85.6 us  [local(): lax.all_gather(down_weight, 'seq', axis=0, tiled=True)]
    all_gather x1, waiting for transfers between devices: 86.2 us -> 92.7 us  [local(): up_sum = add_rows(lax.all_gather(up_weight, 'seq', axis=0, tiled=True))]
  transfers between devices with their start and end apart: 8 -> 8, of which waited for: 5 -> 5; matrix products, arithmetic and copies ran while one was open for 14% -> 12% of each run, Pallas kernels for 0% -> 0%
where the time goes in v1:
time: 572 us; the launch traced here: 571 us
  waiting for transfers between devices  437 us (76%)
  matrix products  68.7 us (12%)
  other arithmetic  26.2 us (5%)
  local copies, waits for them, and re-layouts  18.1 us (3%)
  between operations  13.5 us (2%)
  starting transfers between devices  7.24 us (1%)
    all_gather x1, waiting for transfers between devices, local(): ffn_whole = all_gather(ffn_out, axis_name='ffn').sum(axis=0)  104 us
    all_gather x1, waiting for transfers between devices, local(): gate_sum = add_rows(lax.all_gather(gate_weight, 'seq', axis=0, tiled=True))  95.2 us
    all_gather x1, waiting for transfers between devices, local(): up_sum = add_rows(lax.all_gather(up_weight, 'seq', axis=0, tiled=True))  92.7 us
    all_gather x1, waiting for transfers between devices, local(): lax.all_gather(down_weight, 'seq', axis=0, tiled=True)  85.6 us
    reduce_scatter x1, waiting for transfers between devices, local(): lax.psum_scatter(partial_sum, 'ffn', scatter_dimension=1, tiled=True)  57.5 us
    reduce_sum x1, other arithmetic, local(): ffn_whole = all_gather(ffn_out, axis_name='ffn').sum(axis=0)  14.3 us
    sub x2, matrix products, masked_softmax(): exp_terms = jnp.exp(masked - row_max)  12.8 us
    dot_general x1, matrix products, local(): lax.dot_general(hidden, lax.all_gather(down_weight, 'seq', axis=0, tiled=...  12.1 us
  transfers between devices with their start and end apart: 8, of which 5 were waited for; matrix products, arithmetic and copies ran while one was open for 12% of the time, Pallas kernels for 0%

profile of v1, /device:TPU:1, one launch (start us, length us, event | category | flops | bytes accessed | tf_op | source)
XLA Modules:
  0.0 571.0 jit_solution(16748611505055909145)
XLA Ops:
  6.5 0.7 all-gather.6.cloned.1.call-update
  7.3 0.0 all-gather.10.cloned.1.call-start
  7.3 0.7 all-gather.10.cloned.1.call-update
  8.0 0.0 all-gather.8.cloned.1.call-start
  8.1 0.7 all-gather.8.cloned.1.call-update
  8.7 0.0 all-gather.12.cloned.1.call-start
  8.8 2.1 fusion.7
  10.9 0.0 copy-start.3
  10.9 95.2 %all-gather.6.cloned.1.call-done = bf16[4096,896]{1,0:T(8,128)(2,1)} async-done(((bf16[128,896]{1,0:T(8,128)(2,1)}), bf16[4096,896]{1,0:T(8,128)(2,1)}) %all-gather.6.cloned.1.call-update) | async-done | bytes 7340048 | tf_op jit(solution)/shard_map/all_gather | solution.py:68
  106.1 7.0 %fusion.30 = f32[256,896]{1,0:T(8,128)} fusion(bf16[4096,896]{1,0:T(8,128)(2,1)} %all-gather.6.cloned.1.call-done, bf16[256,4096]{1,0:T(8,128)(2,1)} %param.14, f32[256]{0:T(256)S(1)} %add_rsqrt_fusion), kind=kOutput, calls=%fused_computation.50 | convolution fusion | flops 1882193920 | bytes 10355712 | tf_op jit(solution)/shard_map/dot_general | solution.py:66
  113.1 85.6 %all-gather.10.cloned.1.call-done = bf16[4096,896]{1,0:T(8,128)(2,1)} async-done(((bf16[128,896]{1,0:T(8,128)(2,1)}), bf16[4096,896]{1,0:T(8,128)(2,1)}) %all-gather.10.cloned.1.call-update) | async-done | bytes 7340048 | tf_op jit(solution)/shard_map/all_gather | solution.py:73
  198.8 92.7 %all-gather.8.cloned.1.call-done = bf16[4096,896]{1,0:T(8,128)(2,1)} async-done(((bf16[128,896]{1,0:T(8,128)(2,1)}), bf16[4096,896]{1,0:T(8,128)(2,1)}) %all-gather.8.cloned.1.call-update) | async-done | bytes 7340048 | tf_op jit(solution)/shard_map/all_gather | solution.py:69
  291.4 12.1 %fusion.35 = f32[256,4096]{1,0:T(8,128)} fusion(bf16[4096,896]{1,0:T(8,128)(2,1)} %all-gather.10.cloned.1.call-done, bf16[4096,896]{1,0:T(8,128)(2,1)} %all-gather.8.cloned.1.call-done, f32[256,896]{1,0:T(8,128)} %fusion.30, bf16[256,4096]{1,0:T(8,128)(2,1)S(1)} %copy-done.3, f32[256]{0:T(256)S(1)} %add_rsqrt_fusion), kind=kOutput, calls=%fused_computation.52 | convolution fusion | flops 3762618368 | bytes 21890048 | tf_op jit(solution)/shard_map/dot_general | solution.py:71
  303.5 0.0 all-gather.12.cloned.1.call-update
  303.6 0.0 reduce-scatter.2.cloned.1.call-start
  303.6 0.9 copy-done.13
  304.5 3.8 convolution_convert_fusion.1
  308.4 0.0 copy-start.19
  308.4 1.5 convolution_convert_fusion.2
  309.9 0.8 fusion.38
  310.7 0.1 copy-done.6
  310.8 2.7 collective-permute-start.2
  313.5 4.9 convolution_convert_fusion
  318.4 3.3 reshape.198
  321.8 0.1 add_compare_fusion
  321.9 0.4 fusion.16
  322.3 1.5 and_and_fusion
  323.8 2.2 broadcast_and_fusion
  326.0 4.5 convolution_convert_fusion.3
  330.5 0.0 collective-permute-done.2
  330.5 2.5 pad_maximum_fusion
  333.1 2.7 reshape.191
  335.7 2.6 reshape.192
  338.4 1.6 constant_dynamic-update-slice_fusion.1
  340.0 1.6 constant_dynamic-update-slice_fusion
  341.6 0.7 fusion.51
  342.4 1.3 copy.20
  343.7 1.4 copy.18
  345.0 11.0 %fusion.54 = (f32[4,2,512]{2,1,0:T(2,128)S(1)}, f32[4,2,512,1024]{3,2,1,0:T(8,128)}) fusion(pred[4,512,1024]{2,1,0:T(8,128)(4,1)} %broadcast_and_fusion, bf16[4,1024,2,64]{1,3,2,0:T(8,128)(2,1)} %bitcast.49, bf16[4,512,2,64]{3,2,1,0:T(2,128)(2,1)} %reshape.198), kind=kOutput, calls=%fused_computation.79 | convolution fusion | flops 553649152 | bytes 20463616 | tf_op jit(solution)/shard_map/sub | solution.py:42
  356.0 104.2 %all-gather.12.cloned.1.call-done = f32[2048,4096]{1,0:T(8,128)} async-done(((f32[256,4096]{1,0:T(8,128)}), f32[2048,4096]{1,0:T(8,128)}) %all-gather.12.cloned.1.call-update) | async-done | bytes 33554448 | tf_op jit(solution)/shard_map/all_gather | solution.py:77
  460.2 14.3 %reduce_sum.37 = f32[256,4096]{1,0:T(8,128)} reduce(f32[8,256,4096]{2,1,0:T(8,128)} %bitcast.45, f32[]{:T(128)} %constant.15.clone.1), dimensions={0}, to_apply=%region_1.2 | reduce | flops 7340032 | bytes 37748740 | tf_op jit(solution)/shard_map/reduce_sum | solution.py:77
  474.5 3.1 convolution_convert_fusion.4
  477.7 0.3 copy-done.1
  478.0 0.3 copy-done.8
  478.3 0.9 convolution_convert_fusion.5
  479.2 0.1 fusion.39
  479.2 3.1 collective-permute-start
  482.4 1.3 collective-permute-start.1
  483.7 0.0 copy-start.11
  483.7 8.6 %fusion.21 = bf16[4,512,2,64]{1,3,2,0:T(8,128)(2,1)S(1)} fusion(bf16[4,1024,2,64]{1,3,2,0:T(8,128)(2,1)S(1)} %bitcast.48, f32[4,2,512,1024]{3,2,1,0:T(8,128)} %get-tuple-element.14, f32[4,2,512]{2,1,0:T(2,128)S(1)} %get-tuple-element.13), kind=kOutput, calls=%fused_computation.39 | convolution fusion | flops 545521664 | bytes 18366464 | tf_op jit(solution)/shard_map/bhqk,bkhd->bqhd/dot_general | solution.py:150
  492.3 0.4 copy.22
  492.7 0.1 copy.25
  492.8 0.0 collective-permute-done
  492.9 0.1 pad_maximum_fusion.3
  493.0 0.7 fusion.52
  493.7 1.8 fusion.53
  495.5 0.0 copy-start.16
  495.5 3.5 fusion.15
  499.0 0.0 copy-start.12
  499.1 1.3 fusion.59
  500.3 4.5 convolution_add_fusion
  504.9 0.0 reduce-scatter.2.cloned.1.call-update
  504.9 57.5 %reduce-scatter.2.cloned.1.call-done = f32[2048,128]{1,0:T(8,128)} async-done(((f32[2048,1024]{1,0:T(8,128)}), f32[2048,128]{1,0:T(8,128)}) %reduce-scatter.2.cloned.1.call-update) | async-done | bytes 1048592 | tf_op jit(solution)/shard_map/reduce_scatter | solution.py:157
  562.4 2.1 convert_element_type.68
  (39 shorter events, 0.1 us)
Async XLA Ops:
  6.5 468.0 %copy-start = (bf16[4096,128]{1,0:T(8,128)(2,1)S(1)}, bf16[4096,128]{1,0:T(8,128)(2,1)}, u32[]{:S(2)}) copy-start(bf16[4096,128]{1,0:T(8,128)(2,1)} %param.19) | copy-start | bytes 3145732
  6.5 99.6 %all-gather.6.cloned.1.call-start = ((), (), s32[]{:S(2)}) async-start(), calls=%async_computation.1 | async-start | bytes 7569408 | tf_op jit(solution)/shard_map/all_gather | solution.py:68
  7.3 191.5 %all-gather.10.cloned.1.call-start = ((), (), s32[]{:S(2)}) async-start(), calls=%async_computation.3 | async-start | bytes 7569408 | tf_op jit(solution)/shard_map/all_gather | solution.py:73
  8.0 283.4 %all-gather.8.cloned.1.call-start = ((), (), s32[]{:S(2)}) async-start(), calls=%async_computation.2 | async-start | bytes 7569408 | tf_op jit(solution)/shard_map/all_gather | solution.py:69
  8.7 451.5 %all-gather.12.cloned.1.call-start = ((), (), s32[]{:S(2)}) async-start(), calls=%async_computation.5 | async-start | bytes 37748736 | tf_op jit(solution)/shard_map/all_gather | solution.py:77
  10.9 280.5 %copy-start.3 = (bf16[256,4096]{1,0:T(8,128)(2,1)S(1)}, bf16[256,4096]{1,0:T(8,128)(2,1)}, u32[]{:S(2)}) copy-start(bf16[256,4096]{1,0:T(8,128)(2,1)} %param.14) | copy-start | bytes 6291460
  303.5 0.9 copy-start.13
  303.6 258.8 %reduce-scatter.2.cloned.1.call-start = ((), (), s32[]{:S(2)}) async-start(), calls=%async_computation.4 | async-start | bytes 9437184 | tf_op jit(solution)/shard_map/reduce_scatter | solution.py:157
  304.5 3.9 copy-start.2
  304.5 3.9 copy-start.14
  308.4 1.5 copy-start.4
  308.4 5.1 copy-start.19
  309.9 0.9 copy-start.6
  310.8 11.0 %copy-start.18 = (s32[2048]{0:T(1024)S(1)}, s32[2048]{0:T(1024)}, u32[]{:S(2)}) copy-start(s32[2048]{0:T(1024)} %param.21) | copy-start | bytes 24580
  310.8 19.7 %collective-permute-start.2 = (bf16[512,256]{0,1:T(8,128)(2,1)}, bf16[512,256]{0,1:T(8,128)(2,1)}, u32[]{:S(2)}, u32[]{:S(2)}) collective-permute-start(bf16[512,256]{0,1:T(8,128)(2,1)} %fusion.38), channel_id=1, source_target_pairs={{0,8},{8,16},{16,24},{24,32},{32,40},{40,48},{48,56},{56,64},{64,7... | collective-permute-start | bytes 786440 | tf_op jit(solution)/shard_map/ppermute | solution.py:31
  318.4 7.6 %copy-start.15 = (bf16[1024,128]{1,0:T(8,128)(2,1)S(1)}, bf16[1024,128]{1,0:T(8,128)(2,1)}, u32[]{:S(2)}) copy-start(bf16[1024,128]{1,0:T(8,128)(2,1)} %param.22) | copy-start | bytes 786436
  322.3 8.3 %copy-start.5 = (bf16[2048,128]{0,1:T(8,128)(2,1)S(1)}, bf16[2048,128]{0,1:T(8,128)(2,1)}, u32[]{:S(2)}) copy-start(bf16[2048,128]{0,1:T(8,128)(2,1)} %copy-done.4) | copy-start | bytes 1572868
  322.3 8.3 %copy-start.7 = (bf16[2048,128]{0,1:T(8,128)(2,1)S(1)}, bf16[2048,128]{0,1:T(8,128)(2,1)}, u32[]{:S(2)}) copy-start(bf16[2048,128]{0,1:T(8,128)(2,1)} %copy-done.6) | copy-start | bytes 1572868
  474.5 3.4 copy-start.1
  474.5 3.7 copy-start.8
  478.3 5.4 copy-start.9
  479.2 13.6 %collective-permute-start = (bf16[23,256]{0,1:T(8,128)(2,1)S(1)}, bf16[23,256]{0,1:T(8,128)(2,1)S(1)}, u32[]{:S(2)}, u32[]{:S(2)}) collective-permute-start(bf16[23,256]{0,1:T(8,128)(2,1)S(1)} %get-tuple-element.11), channel_id=1, source_target_pairs={{0,8},{8,16},{16,24},{24,32},{32,40},{40,48},{48,56},{56,64},{64,7... | collective-permute-start | bytes 35336 | tf_op jit(solution)/shard_map/ppermute | solution.py:22
  482.4 10.5 %collective-permute-start.1 = (bf16[23,256]{0,1:T(8,128)(2,1)S(1)}, bf16[23,256]{0,1:T(8,128)(2,1)S(1)}, u32[]{:S(2)}, u32[]{:S(2)}) collective-permute-start(bf16[23,256]{0,1:T(8,128)(2,1)S(1)} %get-tuple-element.12), channel_id=1, source_target_pairs={{8,0},{16,8},{24,16},{32,24},{40,32},{48,40},{56,48},{64,56},{72,6... | collective-permute-start | bytes 35336 | tf_op jit(solution)/shard_map/ppermute | solution.py:23
  483.7 10.0 %copy-start.10 = (pred[2048,302]{0,1:T(8,128)(4,1)S(1)}, pred[2048,302]{0,1:T(8,128)(4,1)}, u32[]{:S(2)}) copy-start(pred[2048,302]{0,1:T(8,128)(4,1)} %and_and_fusion) | copy-start | bytes 1855492
  483.7 10.0 %copy-start.11 = (bf16[2048,128]{0,1:T(8,128)(2,1)S(1)}, bf16[2048,128]{0,1:T(8,128)(2,1)}, u32[]{:S(2)}) copy-start(bf16[2048,128]{0,1:T(8,128)(2,1)} %convolution_convert_fusion.3) | copy-start | bytes 1572868
  493.7 1.9 copy-start.17
  495.5 3.5 copy-start.16
  499.0 1.3 copy-start.12
Sparse Core Ops, SparseCore 0:
  9.9 96.1 all-gather.5
  108.7 90.0 all-gather.9
  201.3 90.0 all-gather.7
  303.7 156.5 all-gather.11
  505.0 57.3 reduce-scatter.1
